TPU v7x, 32 devices: a whole 2x2x4 slice. The times are simulated.
32 devices in a mesh: groups: 2 (over y), tensor: 16 (over z, x, core).
Axes of the slice: x: 2, y: 2, z: 4, core: 2. Of those that a mesh axis runs over, the one named last changes fastest.
Arguments:
- inputs: bfloat16 [256, 8192], P('groups', 'tensor'), parts along dimension 0, may hold values from -6 to 6
- gate_weight: bfloat16 [8192, 28672], P(None, 'tensor'), may hold values from -0.09375 to 0.09375
- up_weight: bfloat16 [8192, 28672], P(None, 'tensor'), may hold values from -0.09375 to 0.09375
- down_weight: bfloat16 [28672, 8192], P('tensor'), may hold values from -0.03125 to 0.03125
- cotangent: bfloat16 [4, 256, 8192], P(None, 'groups', 'tensor'), parts along dimension 1, may hold values from -6 to 6
- threshold_levels: int32 [28672], P('tensor'), may hold values from 4 to 16
- membrane_offsets: int32 [256, 28672], P('groups', 'tensor'), parts along dimension 0, may hold values from 0 to 255
Outputs:
- grad_input: float32 [256, 8192], P('groups', 'tensor'), parts along dimension 0
- grad_threshold: float32 [57344], P(('groups', 'tensor')), parts along dimension 0
There are 2 independent parts, one for each index of `groups`. A program takes and returns all parts, laid end to end along the dimension named above; an argument that names none is the same for every part. Nothing has to cross between parts.
All inputs are finite; a program needn't handle non-finite values.
Results may differ from a plain program's by a relative error of at most 0.0031.
Values may be sent and summed in bfloat16 or wider, within the bound.
No kernel may reach another device: no remote copies, remote signals or barrier semaphores. Data moves between devices by JAX's collectives and lax.ppermute only.
A program may use at most 256 MiB of HBM per device.

v0:
```python
import jax
import jax.numpy as jnp
from jax import lax
from jax.sharding import PartitionSpec as P

slope_gain = 4.0


def transposed_product(left, weight):
    return lax.dot_general(
        left, weight, (((1,), (1,)), ((), ())), preferred_element_type=jnp.float32
    )


def body(
    inputs, gate_weight, up_weight, down_weight, cotangent, threshold_levels, membrane_offsets
):
    step_count = cotangent.shape[0]
    piece = lax.all_gather(inputs, "tensor", axis=1, tiled=True)
    gate = jnp.dot(piece, gate_weight, preferred_element_type=jnp.float32)
    up = jnp.dot(piece, up_weight, preferred_element_type=jnp.float32)
    feedback_all = jnp.einsum(
        "tkd,fd->tkf",
        lax.all_gather(cotangent, "tensor", axis=2, tiled=True),
        down_weight,
        preferred_element_type=jnp.float32,
    )
    theta = threshold_levels.astype(jnp.float32) / 8.0
    sig = jax.nn.sigmoid(gate)
    current = gate * sig * up
    dsilu = sig * (1.0 + gate * (1.0 - sig))
    offset_share = membrane_offsets.astype(jnp.float32) / 256.0
    membrane = theta * offset_share
    spikes = []
    for step in range(step_count):
        pre = membrane + current
        spike = jax.nn.sigmoid(slope_gain * (pre - theta))
        spikes.append(spike)
        membrane = pre - theta * spike
    later = jnp.zeros_like(current)
    grad_threshold = jnp.zeros(theta.shape, jnp.float32)
    collected = []
    for step in range(step_count - 1, -1, -1):
        feedback = feedback_all[step]
        spike = spikes[step]
        dspike = theta * (feedback - later)
        slope = slope_gain * spike * (1.0 - spike)
        dpre = dspike * slope + later
        grad_threshold = grad_threshold + jnp.sum(
            feedback * spike - later * spike - dspike * slope, axis=0
        )
        dgate = (dpre * up * dsilu).astype(jnp.bfloat16)
        dup = (dpre * gate * sig).astype(jnp.bfloat16)
        term = transposed_product(dgate, gate_weight) + transposed_product(dup, up_weight)
        collected.append(lax.psum_scatter(term, "tensor", scatter_dimension=1, tiled=True))
        later = dpre
    grad_threshold = grad_threshold + jnp.sum(later * offset_share, axis=0)
    grad_input = collected[0]
    for part_sum in collected[1:]:
        grad_input = grad_input + part_sum
    return (grad_input, grad_threshold)


def solution(mesh):
    placed = (
        P("groups", "tensor"),
        P(None, "tensor"),
        P(None, "tensor"),
        P("tensor", None),
        P(None, "groups", "tensor"),
        P("tensor"),
        P("groups", "tensor"),
    )
    return jax.shard_map(
        body,
        mesh=mesh,
        in_specs=placed,
        out_specs=(P("groups", "tensor"), P(("groups", "tensor"))),
        check_vma=False,
    )
```

profile of v0, /device:TPU:0, one launch (start us, length us, event | category | flops | bytes accessed | tf_op | source)
XLA Modules:
  0.0 368.1 jit_solution(3617723521399008605)
XLA Ops:
  7.2 0.0 all-gather.5.cloned.1.call-start
  7.2 0.7 all-gather.5.cloned.1.call-update
  7.9 0.0 all-gather.3.cloned.1.call-start
  7.9 0.7 all-gather.3.cloned.1.call-update
  8.6 0.0 reduce-scatter.2.cloned.1.call-start
  8.7 0.7 convert_multiply_fusion
  9.4 0.0 copy-start.3
  9.4 44.7 %all-gather.5.cloned.1.call-done = bf16[128,8192]{1,0:T(8,128)(2,1)} async-done(((bf16[128,512]{1,0:T(8,128)(2,1)}), bf16[128,8192]{1,0:T(8,128)(2,1)}) %all-gather.5.cloned.1.call-update) | async-done | bytes 2097168 | tf_op jit(solution)/shard_map/all_gather | solution.py:19
  54.1 0.0 copy-start.2
  54.1 14.8 %fusion.19 = f32[128,1792]{1,0:T(8,128)S(1)} fusion(bf16[128,8192]{1,0:T(8,128)(2,1)} %all-gather.5.cloned.1.call-done, bf16[8192,1792]{1,0:T(8,128)(2,1)} %param.8), kind=kOutput, calls=%fused_computation.54 | convolution fusion | flops 3758096384 | bytes 32374784 | tf_op jit(solution)/shard_map/dot_general | solution.py:20
  68.9 0.0 copy-done.3
  68.9 0.0 copy-done.2
  68.9 15.9 %add_divide_fusion = (f32[128,1792]{1,0:T(8,128)}, f32[128,1792]{1,0:T(8,128)}, f32[128,1792]{1,0:T(8,128)S(1)}) fusion(f32[1792]{0:T(1024)S(1)} %get-tuple-element.14, f32[1792]{0:T(1024)S(1)} %get-tuple-element.13, s32[128,1792]{1,0:T(8,128)S(1)} %copy-done.3, f32[128,1792]{1,0:T(8,128)S(1)} %fusion.19, bf16[128,8192]{1,0:T(8,128)(2,1)S(1)} %copy-done.2, ...), kind=kOutput, calls=%fused_computation.34 | convolution fusion | flops 3766583296 | bytes 36059136 | tf_op jit(solution)/shard_map/dot_general | solution.py:21
  84.8 48.5 %all-gather.3.cloned.1.call-done = bf16[4,128,8192]{2,1,0:T(8,128)(2,1)} async-done(((bf16[4,128,512]{2,1,0:T(8,128)(2,1)}), bf16[4,128,8192]{2,1,0:T(8,128)(2,1)}) %all-gather.3.cloned.1.call-update) | async-done | bytes 8388624 | tf_op jit(solution)/shard_map/all_gather | solution.py:24
  133.3 0.0 copy-start.4
  133.3 0.0 copy-start.5
  133.3 0.0 copy-start.6
  133.3 23.0 %fusion = f32[4,128,1792]{2,1,0:T(8,128)} fusion(bf16[4,128,8192]{2,1,0:T(8,128)(2,1)} %all-gather.3.cloned.1.call-done, bf16[1792,8192]{1,0:T(8,128)(2,1)} %param.10), kind=kOutput, calls=%fused_computation | convolution fusion | flops 15032385536 | bytes 41418752 | tf_op jit(solution)/shard_map/tkd,fd->tkf/dot_general | solution.py:22
  156.3 0.0 copy-done.4
  156.3 0.0 copy-done.5
  156.3 0.0 copy-done.6
  156.3 4.8 %subtract_reduce_fusion.2 = (f32[1792]{0:T(1024)S(1)}, f32[1792]{0:T(1024)S(1)}, f32[1792]{0:T(1024)S(1)}, f32[1792]{0:T(1024)S(1)}, f32[1792]{0:T(1024)S(1)}, /...) fusion(f32[4,128,1792]{2,1,0:T(8,128)} %fusion, ...), kind=kLoop, calls=%fused_computation.16 | loop fusion | flops 16735488 | bytes 10142720 | tf_op jit(solution)/shard_map/reduce_sum | solution.py:49
  161.0 0.0 copy-start
  161.0 1.0 copy-done
  162.0 14.3 %fusion.11 = f32[128,8192]{1,0:T(8,128)S(1)} fusion(bf16[8192,1792]{1,0:T(8,128)(2,1)} %param.8, f32[128,1792]{1,0:T(8,128)S(1)} %get-tuple-element.7, f32[128,1792]{1,0:T(8,128)S(1)} %get-tuple-element.15, f32[128,1792]{1,0:T(8,128)S(1)} %fusion.19), kind=kOutput, calls=%fused_computation.46 | convolution fusion | flops 3760390144 | bytes 36306944 | tf_op jit(solution)/shard_map/dot_general | solution.py:10
  176.3 15.9 %convolution_add_fusion = f32[128,8192]{1,0:T(8,128)} fusion(f32[128,8192]{1,0:T(8,128)S(1)} %fusion.11, bf16[8192,1792]{1,0:T(8,128)(2,1)} %param.9, f32[128,1792]{1,0:T(8,128)} %copy-done, f32[128,1792]{1,0:T(8,128)S(1)} %fusion.19), kind=kOutput, calls=%fused_computation.2 | convolution fusion | flops 3760521216 | bytes 39583744 | tf_op jit(solution)/shard_map/dot_general | solution.py:10
  192.2 14.4 %fusion.10 = f32[128,8192]{1,0:T(8,128)S(1)} fusion(bf16[8192,1792]{1,0:T(8,128)(2,1)} %param.8, f32[128,1792]{1,0:T(8,128)} %get-tuple-element.8, f32[128,1792]{1,0:T(8,128)S(1)} %get-tuple-element.15, f32[128,1792]{1,0:T(8,128)S(1)} %fusion.19), kind=kOutput, calls=%fused_computation.45 | convolution fusion | flops 3760390144 | bytes 36306944 | tf_op jit(solution)/shard_map/dot_general | solution.py:10
  206.7 16.0 %convolution_add_fusion.1 = f32[128,8192]{1,0:T(8,128)} fusion(f32[128,8192]{1,0:T(8,128)S(1)} %fusion.10, bf16[8192,1792]{1,0:T(8,128)(2,1)} %param.9, f32[128,1792]{1,0:T(8,128)} %get-tuple-element.8, f32[128,1792]{1,0:T(8,128)S(1)} %fusion.19), kind=kOutput, calls=%fused_computation.3 | convolution fusion | flops 3760521216 | bytes 39583744 | tf_op jit(solution)/shard_map/dot_general | solution.py:10
  222.6 14.2 %fusion.9 = f32[128,8192]{1,0:T(8,128)S(1)} fusion(bf16[8192,1792]{1,0:T(8,128)(2,1)} %param.8, f32[128,1792]{1,0:T(8,128)S(1)} %get-tuple-element.9, f32[128,1792]{1,0:T(8,128)S(1)} %get-tuple-element.15, f32[128,1792]{1,0:T(8,128)S(1)} %fusion.19), kind=kOutput, calls=%fused_computation.44 | convolution fusion | flops 3760390144 | bytes 36306944 | tf_op jit(solution)/shard_map/dot_general | solution.py:10
  236.9 16.7 %convolution_add_fusion.2 = f32[128,8192]{1,0:T(8,128)} fusion(f32[128,8192]{1,0:T(8,128)S(1)} %fusion.9, bf16[8192,1792]{1,0:T(8,128)(2,1)} %param.9, f32[128,1792]{1,0:T(8,128)S(1)} %get-tuple-element.9, f32[128,1792]{1,0:T(8,128)S(1)} %fusion.19), kind=kOutput, calls=%fused_computation.4 | convolution fusion | flops 3760521216 | bytes 39583744 | tf_op jit(solution)/shard_map/dot_general | solution.py:10
  253.6 0.0 copy-start.1
  253.6 18.2 %fusion.8 = f32[128,8192]{1,0:T(8,128)} fusion(bf16[8192,1792]{1,0:T(8,128)(2,1)} %param.8, f32[128,1792]{1,0:T(8,128)} %get-tuple-element.10, f32[128,1792]{1,0:T(8,128)S(1)} %get-tuple-element.15, f32[128,1792]{1,0:T(8,128)S(1)} %fusion.19), kind=kOutput, calls=%fused_computation.43 | convolution fusion | flops 3760390144 | bytes 36306944 | tf_op jit(solution)/shard_map/dot_general | solution.py:10
  271.7 0.0 copy-done.1
  271.7 19.2 %fusion.4 = f32[128,8192]{1,0:T(8,128)} fusion(f32[128,8192]{1,0:T(8,128)} %convolution_add_fusion, f32[128,8192]{1,0:T(8,128)} %convolution_add_fusion.1, f32[128,8192]{1,0:T(8,128)} %convolution_add_fusion.2, f32[128,8192]{1,0:T(8,128)} %fusion.8, bf16[8192,1792]{1,0:T(8,128)(2,1)} %param.9, f32[128,1792]{1,0:T(8,128)S(1)} %copy-done.1, ...), kind=kOutput, calls=%fused_computation.8 | convolution fusion | flops 3763666944 | bytes 52166656 | tf_op jit(solution)/shard_map/dot_general | solution.py:10
  290.9 0.0 reduce-scatter.2.cloned.1.call-update
  291.0 0.6 add_add_fusion
  291.6 70.0 %reduce-scatter.2.cloned.1.call-done = f32[128,512]{1,0:T(8,128)} async-done(((f32[128,8192]{1,0:T(8,128)}), f32[128,512]{1,0:T(8,128)}) %reduce-scatter.2.cloned.1.call-update) | async-done | bytes 262160 | tf_op jit(solution)/shard_map/reduce_scatter | solution.py:55
Async XLA Ops:
  7.2 46.9 %all-gather.5.cloned.1.call-start = ((), (), s32[]{:S(2)}) async-start(), calls=%async_computation.2 | async-start | bytes 2228224 | tf_op jit(solution)/shard_map/all_gather | solution.py:19
  7.9 125.4 %all-gather.3.cloned.1.call-start = ((), (), s32[]{:S(2)}) async-start(), calls=%async_computation.1 | async-start | bytes 8912896 | tf_op jit(solution)/shard_map/all_gather | solution.py:24
  8.6 353.0 %reduce-scatter.2.cloned.1.call-start = ((), (), s32[]{:S(2)}) async-start(), calls=%async_computation.3 | async-start | bytes 4456448 | tf_op jit(solution)/shard_map/reduce_scatter | solution.py:55
  9.4 59.5 %copy-start.3 = (s32[128,1792]{1,0:T(8,128)S(1)}, s32[128,1792]{1,0:T(8,128)}, u32[]{:S(2)}) copy-start(s32[128,1792]{1,0:T(8,128)} %param.13) | copy-start | bytes 2752516
  54.1 14.8 %copy-start.2 = (bf16[128,8192]{1,0:T(8,128)(2,1)S(1)}, bf16[128,8192]{1,0:T(8,128)(2,1)}, u32[]{:S(2)}) copy-start(bf16[128,8192]{1,0:T(8,128)(2,1)} %all-gather.5.cloned.1.call-done) | copy-start | bytes 6291460
  133.3 23.0 %copy-start.4 = (s32[128,1792]{1,0:T(8,128)S(1)}, s32[128,1792]{1,0:T(8,128)}, u32[]{:S(2)}) copy-start(s32[128,1792]{1,0:T(8,128)} %param.13) | copy-start | bytes 2752516
  133.3 23.0 %copy-start.5 = (f32[128,1792]{1,0:T(8,128)S(1)}, f32[128,1792]{1,0:T(8,128)}, u32[]{:S(2)}) copy-start(f32[128,1792]{1,0:T(8,128)} %get-tuple-element.11) | copy-start | bytes 2752516
  133.3 23.0 %copy-start.6 = (f32[128,1792]{1,0:T(8,128)S(1)}, f32[128,1792]{1,0:T(8,128)}, u32[]{:S(2)}) copy-start(f32[128,1792]{1,0:T(8,128)} %get-tuple-element.12) | copy-start | bytes 2752516
  161.0 1.0 copy-start
  253.6 18.2 %copy-start.1 = (f32[128,1792]{1,0:T(8,128)S(1)}, f32[128,1792]{1,0:T(8,128)}, u32[]{:S(2)}) copy-start(f32[128,1792]{1,0:T(8,128)} %get-tuple-element.10) | copy-start | bytes 2752516
Sparse Core Ops, SparseCore 0:
  10.2 43.8 all-gather.4
  56.2 77.0 all-gather.2
  291.1 70.4 reduce-scatter.1
where the time goes:
time: 369 us; the launch traced here: 368 us
  matrix products  183 us (50%)
  waiting for transfers between devices  165 us (45%)
  between operations  13.8 us (4%)
  other arithmetic  6.08 us (2%)
    dot_general x8, matrix products, transposed_product(): lax.dot_general(left, weight, (((1,), (1,)), ((), ())), preferred_element...  129 us
    reduce_scatter x1, waiting for transfers between devices, body(): lax.psum_scatter(term, 'tensor', scatter_dimension=1, tiled=True)  70 us
    all_gather x1, waiting for transfers between devices, body(): lax.all_gather(cotangent, 'tensor', axis=2, tiled=True)  48.5 us
    all_gather x1, waiting for transfers between devices, body(): piece = lax.all_gather(inputs, 'tensor', axis=1, tiled=True)  44.7 us
    dot_general x1, matrix products, body(): jnp.einsum('tkd,fd->tkf', lax.all_gather(cotangent, 'tensor', axis=2, til...  23 us
    dot_general x1, matrix products, body(): up = jnp.dot(piece, up_weight, preferred_element_type=jnp.float32)  15.9 us
    dot_general x1, matrix products, body(): gate = jnp.dot(piece, gate_weight, preferred_element_type=jnp.float32)  14.8 us
  transfers between devices with their start and end apart: 3, of which 3 were waited for; matrix products, arithmetic and copies ran while one was open for 9% of the time, Pallas kernels for 0%

commit v1 on v0

--- a/solution.py
+++ b/solution.py
@@ -4,6 +4,19 @@
 from jax.sharding import PartitionSpec as P
 
 slope_gain = 4.0
+
+
+def collect(x, axis, dim):
+    ways = lax.axis_size(axis)
+    up = [(d, (d + 1) % ways) for d in range(ways)]
+    down = [(d, (d - 1) % ways) for d in range(ways)]
+    earlier, later = ([x], [x])
+    for _ in range(ways // 2):
+        earlier.append(lax.ppermute(earlier[-1], axis, up))
+    for _ in range((ways - 1) // 2):
+        later.append(lax.ppermute(later[-1], axis, down))
+    line = jnp.concatenate([*earlier[::-1], *later[1:]], axis=dim)
+    return jnp.roll(line, (lax.axis_index(axis) - ways // 2) * x.shape[dim], axis=dim)
 
 
 def transposed_product(left, weight):
@@ -21,7 +34,7 @@
     up = jnp.dot(piece, up_weight, preferred_element_type=jnp.float32)
     feedback_all = jnp.einsum(
         "tkd,fd->tkf",
-        lax.all_gather(cotangent, "tensor", axis=2, tiled=True),
+        collect(cotangent, "tensor", 2),
         down_weight,
         preferred_element_type=jnp.float32,
     )

time: 369 us -> 415 us (1.12)
  starting transfers between devices: 0.11 us -> 69.3 us
  waiting for transfers between devices: 165 us -> 109 us
  local copies, waits for them, and re-layouts: 1.01 us -> 37.4 us
  matrix products: 183 us -> 178 us
    ppermute x0 -> x15, starting transfers between devices: none -> 69.2 us  [the longest x8 60.3 us: collect(): earlier.append(lax.ppermute(earlier[-1], axis, up))]
    all_gather x1 -> x0, waiting for transfers between devices: 48.5 us -> none  [body(): lax.all_gather(cotangent, 'tensor', axis=2, tiled=True)]
    all_gather x1, waiting for transfers between devices: 44.7 us -> 0.01 us  [body(): piece = lax.all_gather(inputs, 'tensor', axis=1, tiled=True)]
    unnamed x14 -> x73, local copies, waits for them, and re-layouts: 1.01 us -> 35.5 us
    ppermute x0 -> x15, waiting for transfers between devices: none -> 33.4 us  [the longest x8 33.4 us: collect(): earlier.append(lax.ppermute(earlier[-1], axis, up))]
    reduce_scatter x1, waiting for transfers between devices: 70 us -> 74.9 us  [body(): lax.psum_scatter(term, 'tensor', scatter_dimension=1, tiled=True)]
  transfers between devices with their start and end apart: 3 -> 17, of which waited for: 3 -> 8; matrix products, arithmetic and copies ran while one was open for 9% -> 11% of each run, Pallas kernels for 0% -> 0%
where the time goes in v1:
time: 415 us
  matrix products  178 us (43%)
  waiting for transfers between devices  109 us (26%)
  starting transfers between devices  69.3 us (17%)
  local copies, waits for them, and re-layouts  37.4 us (9%)
  between operations  14.2 us (3%)
  other arithmetic  6.67 us (2%)
    dot_general x8, matrix products, transposed_product(): lax.dot_general(left, weight, (((1,), (1,)), ((), ())), preferred_element...  127 us
    reduce_scatter x1, waiting for transfers between devices, body(): lax.psum_scatter(term, 'tensor', scatter_dimension=1, tiled=True)  74.9 us
    ppermute x8, starting transfers between devices, collect(): earlier.append(lax.ppermute(earlier[-1], axis, up))  60.3 us
    unnamed x73, local copies, waits for them, and re-layouts  35.5 us
    ppermute x8, waiting for transfers between devices, collect(): earlier.append(lax.ppermute(earlier[-1], axis, up))  33.4 us
    dot_general x1, matrix products, body(): jnp.einsum('tkd,fd->tkf', collect(cotangent, 'tensor', 2), down_weight, p...  22.8 us
    dot_general x1, matrix products, body(): up = jnp.dot(piece, up_weight, preferred_element_type=jnp.float32)  15.8 us
    dot_general x1, matrix products, body(): gate = jnp.dot(piece, gate_weight, preferred_element_type=jnp.float32)  12.5 us
  transfers between devices with their start and end apart: 17, of which 8 were waited for; matrix products, arithmetic and copies ran while one was open for 11% of the time, Pallas kernels for 0%

profile of v1, /device:TPU:0, one launch (start us, length us, event | category | flops | bytes accessed | tf_op | source)
XLA Modules:
  0.0 414.6 jit_solution(3703976675616071929)
XLA Ops:
  8.4 5.0 %collective-permute-start.8 = (bf16[4,128,512]{2,1,0:T(8,128)(2,1)}, bf16[4,128,512]{2,1,0:T(8,128)(2,1)S(1)}, u32[]{:S(2)}, u32[]{:S(2)}) collective-permute-start(bf16[4,128,512]{2,1,0:T(8,128)(2,1)} %param.11), channel_id=1, source_target_pairs={{0,15},{1,0},{2,1},{3,2},{4,3},{5,4},{6,5},{7,6},{8,7},{9,8},{10,9... | collective-permute-start | bytes 1572872 | tf_op jit(solution)/shard_map/ppermute | solution.py:17
  13.5 7.1 %collective-permute-done = bf16[4,128,512]{2,1,0:T(8,128)(2,1)S(1)} collective-permute-done((bf16[4,128,512]{2,1,0:T(8,128)(2,1)}, bf16[4,128,512]{2,1,0:T(8,128)(2,1)S(1)}, u32[]{:S(2)}, u32[]{:S(2)}) %collective-permute-start) | collective-permute-done | bytes 524320 | tf_op jit(solution)/shard_map/ppermute | solution.py:15
  20.6 3.9 collective-permute-start.1
  25.1 11.0 %collective-permute-done.1 = bf16[4,128,512]{2,1,0:T(8,128)(2,1)S(1)} collective-permute-done((bf16[4,128,512]{2,1,0:T(8,128)(2,1)S(1)}, bf16[4,128,512]{2,1,0:T(8,128)(2,1)S(1)}, u32[]{:S(2)}, u32[]{:S(2)}) %collective-permute-start.1) | collective-permute-done | bytes 524320 | tf_op jit(solution)/shard_map/ppermute | solution.py:15
  36.1 1.8 collective-permute-start.2
  38.0 2.6 collective-permute-start.10
  40.6 7.0 %collective-permute-done.2 = bf16[4,128,512]{2,1,0:T(8,128)(2,1)S(1)} collective-permute-done((bf16[4,128,512]{2,1,0:T(8,128)(2,1)S(1)}, bf16[4,128,512]{2,1,0:T(8,128)(2,1)S(1)}, u32[]{:S(2)}, u32[]{:S(2)}) %collective-permute-start.2) | collective-permute-done | bytes 524320 | tf_op jit(solution)/shard_map/ppermute | solution.py:15
  47.6 9.5 %collective-permute-start.3 = (bf16[4,128,512]{2,1,0:T(8,128)(2,1)S(1)}, bf16[4,128,512]{2,1,0:T(8,128)(2,1)S(1)}, u32[]{:S(2)}, u32[]{:S(2)}) collective-permute-start(bf16[4,128,512]{2,1,0:T(8,128)(2,1)S(1)} %collective-permute-done.2), channel_id=1, source_target_pairs={{0,1},{1,2},{2,3},{3,4},{4,5},{5,6},{6,7},{7,8},{8,9},{9,10},{10,1... | collective-permute-start | bytes 1572872 | tf_op jit(solution)/shard_map/ppermute | solution.py:15
  57.1 0.7 copy-done.6
  57.9 4.0 collective-permute-done.3
  61.9 8.9 %collective-permute-start.4 = (bf16[4,128,512]{2,1,0:T(8,128)(2,1)S(1)}, bf16[4,128,512]{2,1,0:T(8,128)(2,1)S(1)}, u32[]{:S(2)}, u32[]{:S(2)}) collective-permute-start(bf16[4,128,512]{2,1,0:T(8,128)(2,1)S(1)} %collective-permute-done.3), channel_id=1, source_target_pairs={{0,1},{1,2},{2,3},{3,4},{4,5},{5,6},{6,7},{7,8},{8,9},{9,10},{10,1... | collective-permute-start | bytes 1572872 | tf_op jit(solution)/shard_map/ppermute | solution.py:15
  71.6 1.8 collective-permute-done.4
  73.4 10.6 %collective-permute-start.5 = (bf16[4,128,512]{2,1,0:T(8,128)(2,1)S(1)}, bf16[4,128,512]{2,1,0:T(8,128)(2,1)S(1)}, u32[]{:S(2)}, u32[]{:S(2)}) collective-permute-start(bf16[4,128,512]{2,1,0:T(8,128)(2,1)S(1)} %collective-permute-done.4), channel_id=1, source_target_pairs={{0,1},{1,2},{2,3},{3,4},{4,5},{5,6},{6,7},{7,8},{8,9},{9,10},{10,1... | collective-permute-start | bytes 1572872 | tf_op jit(solution)/shard_map/ppermute | solution.py:15
  84.1 1.5 collective-permute-done.5
  85.6 12.7 %collective-permute-start.6 = (bf16[4,128,512]{2,1,0:T(8,128)(2,1)S(1)}, bf16[4,128,512]{2,1,0:T(8,128)(2,1)}, u32[]{:S(2)}, u32[]{:S(2)}) collective-permute-start(bf16[4,128,512]{2,1,0:T(8,128)(2,1)S(1)} %collective-permute-done.5), channel_id=1, source_target_pairs={{0,1},{1,2},{2,3},{3,4},{4,5},{5,6},{6,7},{7,8},{8,9},{9,10},{10,1... | collective-permute-start | bytes 1572872 | tf_op jit(solution)/shard_map/ppermute | solution.py:15
  98.2 0.7 convert_multiply_fusion
  99.0 1.0 collective-permute-done.6
  99.9 12.4 %collective-permute-start.7 = (bf16[4,128,512]{2,1,0:T(8,128)(2,1)}, bf16[4,128,512]{2,1,0:T(8,128)(2,1)}, u32[]{:S(2)}, u32[]{:S(2)}) collective-permute-start(bf16[4,128,512]{2,1,0:T(8,128)(2,1)} %collective-permute-done.6), channel_id=1, source_target_pairs={{0,1},{1,2},{2,3},{3,4},{4,5},{5,6},{6,7},{7,8},{8,9},{9,10},{10,1... | collective-permute-start | bytes 1572872 | tf_op jit(solution)/shard_map/ppermute | solution.py:15
  112.3 12.5 %fusion.21 = f32[128,1792]{1,0:T(8,128)S(1)} fusion(bf16[128,8192]{1,0:T(8,128)(2,1)} %all-gather.2.cloned.1.call-done, bf16[8192,1792]{1,0:T(8,128)(2,1)} %param.8), kind=kOutput, calls=%fused_computation.88 | convolution fusion | flops 3758096384 | bytes 32374784 | tf_op jit(solution)/shard_map/dot_general | solution.py:33
  124.9 15.8 %add_divide_fusion = (f32[128,1792]{1,0:T(8,128)}, f32[128,1792]{1,0:T(8,128)}, f32[128,1792]{1,0:T(8,128)S(1)}) fusion(f32[1792]{0:T(1024)S(1)} %get-tuple-element.14, f32[1792]{0:T(1024)S(1)} %get-tuple-element.13, s32[128,1792]{1,0:T(8,128)S(1)} %copy-done.20, f32[128,1792]{1,0:T(8,128)S(1)} %fusion.21, bf16[128,8192]{1,0:T(8,128)(2,1)S(1)} %copy-done.2, ...), kind=kOutput, calls=%fused_computation.35 | convolution fusion | flops 3766583296 | bytes 36059136 | tf_op jit(solution)/shard_map/dot_general | solution.py:34
  140.7 1.9 constant_dynamic-update-slice_fusion.31
  142.6 1.9 constant_dynamic-update-slice_fusion.30
  144.5 0.8 constant_dynamic-update-slice_fusion.29
  145.3 0.8 constant_dynamic-update-slice_fusion.28
  146.1 0.9 constant_dynamic-update-slice_fusion.27
  147.0 0.8 constant_dynamic-update-slice_fusion.26
  147.8 0.8 constant_dynamic-update-slice_fusion.25
  148.7 0.8 constant_dynamic-update-slice_fusion.24
  149.5 0.9 constant_dynamic-update-slice_fusion.23
  150.4 0.8 constant_dynamic-update-slice_fusion.22
  151.2 0.8 constant_dynamic-update-slice_fusion.21
  152.1 0.9 constant_dynamic-update-slice_fusion.20
  152.9 0.8 constant_dynamic-update-slice_fusion.19
  153.8 0.9 constant_dynamic-update-slice_fusion.18
  154.6 1.9 constant_dynamic-update-slice_fusion.17
  156.5 1.9 constant_dynamic-update-slice_fusion.16
  158.4 1.9 constant_dynamic-update-slice_fusion.15
  160.3 1.9 constant_dynamic-update-slice_fusion.14
  162.2 0.8 constant_dynamic-update-slice_fusion.13
  163.1 0.8 constant_dynamic-update-slice_fusion.12
  163.9 0.8 constant_dynamic-update-slice_fusion.11
  164.7 0.8 constant_dynamic-update-slice_fusion.10
  165.6 0.9 constant_dynamic-update-slice_fusion.9
  166.4 0.9 constant_dynamic-update-slice_fusion.8
  167.3 0.9 constant_dynamic-update-slice_fusion.7
  168.2 0.9 constant_dynamic-update-slice_fusion.6
  169.0 0.9 constant_dynamic-update-slice_fusion.5
  169.9 0.9 constant_dynamic-update-slice_fusion.4
  170.7 0.9 constant_dynamic-update-slice_fusion.3
  171.6 0.8 constant_dynamic-update-slice_fusion.2
  172.4 1.9 constant_dynamic-update-slice_fusion.1
  174.3 1.9 constant_dynamic-update-slice_fusion
  176.2 22.8 %fusion = f32[4,128,1792]{2,1,0:T(8,128)} fusion(bf16[1792,8192]{1,0:T(8,128)(2,1)} %param.10, bf16[4,128,16384]{2,1,0:T(8,128)(2,1)} %constant_dynamic-update-slice_fusion, s32[]{:T(128)S(6)} %select_n.14), kind=kOutput, calls=%fused_computation | convolution fusion | flops 15032385536 | bytes 41418756 | tf_op jit(solution)/shard_map/tkd,fd->tkf/dot_general | solution.py:35
  199.0 5.4 %subtract_reduce_fusion.2 = (f32[1792]{0:T(1024)S(1)}, f32[1792]{0:T(1024)S(1)}, f32[1792]{0:T(1024)S(1)}, f32[1792]{0:T(1024)S(1)}, f32[1792]{0:T(1024)S(1)}, /...) fusion(f32[4,128,1792]{2,1,0:T(8,128)} %fusion, ...), kind=kLoop, calls=%fused_computation.17 | loop fusion | flops 16735488 | bytes 10142720 | tf_op jit(solution)/shard_map/reduce_sum | solution.py:62
  204.4 0.9 copy-done
  205.3 14.3 %fusion.10 = f32[128,8192]{1,0:T(8,128)S(1)} fusion(bf16[8192,1792]{1,0:T(8,128)(2,1)} %param.8, f32[128,1792]{1,0:T(8,128)S(1)} %get-tuple-element.9, f32[128,1792]{1,0:T(8,128)S(1)} %get-tuple-element.15, f32[128,1792]{1,0:T(8,128)S(1)} %fusion.21), kind=kOutput, calls=%fused_computation.45 | convolution fusion | flops 3760390144 | bytes 36306944 | tf_op jit(solution)/shard_map/dot_general | solution.py:23
  219.6 15.9 %convolution_add_fusion.2 = f32[128,8192]{1,0:T(8,128)} fusion(f32[128,8192]{1,0:T(8,128)S(1)} %fusion.10, bf16[8192,1792]{1,0:T(8,128)(2,1)} %param.9, f32[128,1792]{1,0:T(8,128)} %copy-done, f32[128,1792]{1,0:T(8,128)S(1)} %fusion.21), kind=kOutput, calls=%fused_computation.4 | convolution fusion | flops 3760521216 | bytes 39583744 | tf_op jit(solution)/shard_map/dot_general | solution.py:23
  235.5 14.5 %fusion.11 = f32[128,8192]{1,0:T(8,128)S(1)} fusion(bf16[8192,1792]{1,0:T(8,128)(2,1)} %param.8, f32[128,1792]{1,0:T(8,128)} %get-tuple-element.8, f32[128,1792]{1,0:T(8,128)S(1)} %get-tuple-element.15, f32[128,1792]{1,0:T(8,128)S(1)} %fusion.21), kind=kOutput, calls=%fused_computation.46 | convolution fusion | flops 3760390144 | bytes 36306944 | tf_op jit(solution)/shard_map/dot_general | solution.py:23
  250.0 15.9 %convolution_add_fusion.1 = f32[128,8192]{1,0:T(8,128)} fusion(f32[128,8192]{1,0:T(8,128)S(1)} %fusion.11, bf16[8192,1792]{1,0:T(8,128)(2,1)} %param.9, f32[128,1792]{1,0:T(8,128)} %get-tuple-element.8, f32[128,1792]{1,0:T(8,128)S(1)} %fusion.21), kind=kOutput, calls=%fused_computation.3 | convolution fusion | flops 3760521216 | bytes 39583744 | tf_op jit(solution)/shard_map/dot_general | solution.py:23
  265.9 15.5 %fusion.9 = f32[128,8192]{1,0:T(8,128)} fusion(bf16[8192,1792]{1,0:T(8,128)(2,1)} %param.8, f32[128,1792]{1,0:T(8,128)} %get-tuple-element.10, f32[128,1792]{1,0:T(8,128)S(1)} %get-tuple-element.15, f32[128,1792]{1,0:T(8,128)S(1)} %fusion.21), kind=kOutput, calls=%fused_computation.44 | convolution fusion | flops 3760390144 | bytes 36306944 | tf_op jit(solution)/shard_map/dot_general | solution.py:23
  281.5 14.2 %fusion.12 = f32[128,8192]{1,0:T(8,128)S(1)} fusion(bf16[8192,1792]{1,0:T(8,128)(2,1)} %param.8, f32[128,1792]{1,0:T(8,128)S(1)} %get-tuple-element.7, f32[128,1792]{1,0:T(8,128)S(1)} %get-tuple-element.15, f32[128,1792]{1,0:T(8,128)S(1)} %fusion.21), kind=kOutput, calls=%fused_computation.47 | convolution fusion | flops 3760390144 | bytes 36306944 | tf_op jit(solution)/shard_map/dot_general | solution.py:23
  295.7 17.2 %convolution_add_fusion = f32[128,8192]{1,0:T(8,128)} fusion(f32[128,8192]{1,0:T(8,128)S(1)} %fusion.12, bf16[8192,1792]{1,0:T(8,128)(2,1)} %param.9, f32[128,1792]{1,0:T(8,128)S(1)} %get-tuple-element.7, f32[128,1792]{1,0:T(8,128)S(1)} %fusion.21), kind=kOutput, calls=%fused_computation.2 | convolution fusion | flops 3760521216 | bytes 39583744 | tf_op jit(solution)/shard_map/dot_general | solution.py:23
  312.9 19.3 %fusion.4 = f32[128,8192]{1,0:T(8,128)} fusion(f32[128,8192]{1,0:T(8,128)} %convolution_add_fusion, f32[128,8192]{1,0:T(8,128)} %convolution_add_fusion.1, f32[128,8192]{1,0:T(8,128)} %convolution_add_fusion.2, f32[128,8192]{1,0:T(8,128)} %fusion.9, bf16[8192,1792]{1,0:T(8,128)(2,1)} %param.9, f32[128,1792]{1,0:T(8,128)S(1)} %copy-done.1, ...), kind=kOutput, calls=%fused_computation.8 | convolution fusion | flops 3763666944 | bytes 52166656 | tf_op jit(solution)/shard_map/dot_general | solution.py:23
  332.8 74.9 %reduce-scatter.2.cloned.1.call-done = f32[128,512]{1,0:T(8,128)} async-done(((f32[128,8192]{1,0:T(8,128)}), f32[128,512]{1,0:T(8,128)}) %reduce-scatter.2.cloned.1.call-update) | async-done | bytes 262160 | tf_op jit(solution)/shard_map/reduce_scatter | solution.py:68
  (60 shorter events, 3.5 us)
Async XLA Ops:
  7.2 105.1 %all-gather.2.cloned.1.call-start = ((), (), s32[]{:S(2)}) async-start(), calls=%async_computation.1 | async-start | bytes 2228224 | tf_op jit(solution)/shard_map/all_gather | solution.py:32
  7.9 399.9 %reduce-scatter.2.cloned.1.call-start = ((), (), s32[]{:S(2)}) async-start(), calls=%async_computation.2 | async-start | bytes 4456448 | tf_op jit(solution)/shard_map/reduce_scatter | solution.py:68
  7.9 12.7 %collective-permute-start = (bf16[4,128,512]{2,1,0:T(8,128)(2,1)}, bf16[4,128,512]{2,1,0:T(8,128)(2,1)S(1)}, u32[]{:S(2)}, u32[]{:S(2)}) collective-permute-start(bf16[4,128,512]{2,1,0:T(8,128)(2,1)} %param.11), channel_id=1, source_target_pairs={{0,1},{1,2},{2,3},{3,4},{4,5},{5,6},{6,7},{7,8},{8,9},{9,10},{10,1... | collective-permute-start | bytes 1572872 | tf_op jit(solution)/shard_map/ppermute | solution.py:15
  8.4 16.1 %collective-permute-start.8 = (bf16[4,128,512]{2,1,0:T(8,128)(2,1)}, bf16[4,128,512]{2,1,0:T(8,128)(2,1)S(1)}, u32[]{:S(2)}, u32[]{:S(2)}) collective-permute-start(bf16[4,128,512]{2,1,0:T(8,128)(2,1)} %param.11), channel_id=1, source_target_pairs={{0,15},{1,0},{2,1},{3,2},{4,3},{5,4},{6,5},{7,6},{8,7},{9,8},{10,9... | collective-permute-start | bytes 1572872 | tf_op jit(solution)/shard_map/ppermute | solution.py:17
  20.6 15.5 %collective-permute-start.1 = (bf16[4,128,512]{2,1,0:T(8,128)(2,1)S(1)}, bf16[4,128,512]{2,1,0:T(8,128)(2,1)S(1)}, u32[]{:S(2)}, u32[]{:S(2)}) collective-permute-start(bf16[4,128,512]{2,1,0:T(8,128)(2,1)S(1)} %collective-permute-done), channel_id=1, source_target_pairs={{0,1},{1,2},{2,3},{3,4},{4,5},{5,6},{6,7},{7,8},{8,9},{9,10},{10,1... | collective-permute-start | bytes 1572872 | tf_op jit(solution)/shard_map/ppermute | solution.py:15
  24.5 13.5 %collective-permute-start.9 = (bf16[4,128,512]{2,1,0:T(8,128)(2,1)S(1)}, bf16[4,128,512]{2,1,0:T(8,128)(2,1)S(1)}, u32[]{:S(2)}, u32[]{:S(2)}) collective-permute-start(bf16[4,128,512]{2,1,0:T(8,128)(2,1)S(1)} %collective-permute-done.8), channel_id=1, source_target_pairs={{0,15},{1,0},{2,1},{3,2},{4,3},{5,4},{6,5},{7,6},{8,7},{9,8},{10,9... | collective-permute-start | bytes 1572872 | tf_op jit(solution)/shard_map/ppermute | solution.py:17
  36.1 20.9 %copy-start.4 = (bf16[4,128,512]{2,1,0:T(8,128)(2,1)}, bf16[4,128,512]{2,1,0:T(8,128)(2,1)S(1)}, u32[]{:S(2)}) copy-start(bf16[4,128,512]{2,1,0:T(8,128)(2,1)S(1)} %collective-permute-done.1) | copy-start | bytes 1572868
  36.1 11.4 %collective-permute-start.2 = (bf16[4,128,512]{2,1,0:T(8,128)(2,1)S(1)}, bf16[4,128,512]{2,1,0:T(8,128)(2,1)S(1)}, u32[]{:S(2)}, u32[]{:S(2)}) collective-permute-start(bf16[4,128,512]{2,1,0:T(8,128)(2,1)S(1)} %collective-permute-done.1), channel_id=1, source_target_pairs={{0,1},{1,2},{2,3},{3,4},{4,5},{5,6},{6,7},{7,8},{8,9},{9,10},{10,1... | collective-permute-start | bytes 1572872 | tf_op jit(solution)/shard_map/ppermute | solution.py:15
  38.0 19.1 %collective-permute-start.10 = (bf16[4,128,512]{2,1,0:T(8,128)(2,1)S(1)}, bf16[4,128,512]{2,1,0:T(8,128)(2,1)S(1)}, u32[]{:S(2)}, u32[]{:S(2)}) collective-permute-start(bf16[4,128,512]{2,1,0:T(8,128)(2,1)S(1)} %collective-permute-done.9), channel_id=1, source_target_pairs={{0,15},{1,0},{2,1},{3,2},{4,3},{5,4},{6,5},{7,6},{8,7},{9,8},{10,9... | collective-permute-start | bytes 1572872 | tf_op jit(solution)/shard_map/ppermute | solution.py:17
  47.6 23.2 %copy-start.8 = (bf16[4,128,512]{2,1,0:T(8,128)(2,1)}, bf16[4,128,512]{2,1,0:T(8,128)(2,1)S(1)}, u32[]{:S(2)}) copy-start(bf16[4,128,512]{2,1,0:T(8,128)(2,1)S(1)} %collective-permute-done.2) | copy-start | bytes 1572868
  47.6 14.3 %collective-permute-start.3 = (bf16[4,128,512]{2,1,0:T(8,128)(2,1)S(1)}, bf16[4,128,512]{2,1,0:T(8,128)(2,1)S(1)}, u32[]{:S(2)}, u32[]{:S(2)}) collective-permute-start(bf16[4,128,512]{2,1,0:T(8,128)(2,1)S(1)} %collective-permute-done.2), channel_id=1, source_target_pairs={{0,1},{1,2},{2,3},{3,4},{4,5},{5,6},{6,7},{7,8},{8,9},{9,10},{10,1... | collective-permute-start | bytes 1572872 | tf_op jit(solution)/shard_map/ppermute | solution.py:15
  57.1 0.8 copy-start.6
  57.1 13.7 %collective-permute-start.11 = (bf16[4,128,512]{2,1,0:T(8,128)(2,1)S(1)}, bf16[4,128,512]{2,1,0:T(8,128)(2,1)S(1)}, u32[]{:S(2)}, u32[]{:S(2)}) collective-permute-start(bf16[4,128,512]{2,1,0:T(8,128)(2,1)S(1)} %collective-permute-done.10), channel_id=1, source_target_pairs={{0,15},{1,0},{2,1},{3,2},{4,3},{5,4},{6,5},{7,6},{8,7},{9,8},{10,9... | collective-permute-start | bytes 1572872 | tf_op jit(solution)/shard_map/ppermute | solution.py:17
  61.9 50.4 %copy-start.14 = (bf16[4,128,512]{2,1,0:T(8,128)(2,1)}, bf16[4,128,512]{2,1,0:T(8,128)(2,1)S(1)}, u32[]{:S(2)}) copy-start(bf16[4,128,512]{2,1,0:T(8,128)(2,1)S(1)} %collective-permute-done.3) | copy-start | bytes 1572868
  61.9 11.5 %collective-permute-start.4 = (bf16[4,128,512]{2,1,0:T(8,128)(2,1)S(1)}, bf16[4,128,512]{2,1,0:T(8,128)(2,1)S(1)}, u32[]{:S(2)}, u32[]{:S(2)}) collective-permute-start(bf16[4,128,512]{2,1,0:T(8,128)(2,1)S(1)} %collective-permute-done.3), channel_id=1, source_target_pairs={{0,1},{1,2},{2,3},{3,4},{4,5},{5,6},{6,7},{7,8},{8,9},{9,10},{10,1... | collective-permute-start | bytes 1572872 | tf_op jit(solution)/shard_map/ppermute | solution.py:15
  70.8 0.8 copy-start.10
  70.8 13.2 %collective-permute-start.12 = (bf16[4,128,512]{2,1,0:T(8,128)(2,1)S(1)}, bf16[4,128,512]{2,1,0:T(8,128)(2,1)S(1)}, u32[]{:S(2)}, u32[]{:S(2)}) collective-permute-start(bf16[4,128,512]{2,1,0:T(8,128)(2,1)S(1)} %collective-permute-done.11), channel_id=1, source_target_pairs={{0,15},{1,0},{2,1},{3,2},{4,3},{5,4},{6,5},{7,6},{8,7},{9,8},{10,9... | collective-permute-start | bytes 1572872 | tf_op jit(solution)/shard_map/ppermute | solution.py:17
  73.4 10.6 %copy-start.16 = (bf16[4,128,512]{2,1,0:T(8,128)(2,1)}, bf16[4,128,512]{2,1,0:T(8,128)(2,1)S(1)}, u32[]{:S(2)}) copy-start(bf16[4,128,512]{2,1,0:T(8,128)(2,1)S(1)} %collective-permute-done.4) | copy-start | bytes 1572868
  73.4 12.2 %collective-permute-start.5 = (bf16[4,128,512]{2,1,0:T(8,128)(2,1)S(1)}, bf16[4,128,512]{2,1,0:T(8,128)(2,1)S(1)}, u32[]{:S(2)}, u32[]{:S(2)}) collective-permute-start(bf16[4,128,512]{2,1,0:T(8,128)(2,1)S(1)} %collective-permute-done.4), channel_id=1, source_target_pairs={{0,1},{1,2},{2,3},{3,4},{4,5},{5,6},{6,7},{7,8},{8,9},{9,10},{10,1... | collective-permute-start | bytes 1572872 | tf_op jit(solution)/shard_map/ppermute | solution.py:15
  84.0 28.2 %copy-start.12 = (bf16[4,128,512]{2,1,0:T(8,128)(2,1)}, bf16[4,128,512]{2,1,0:T(8,128)(2,1)S(1)}, u32[]{:S(2)}) copy-start(bf16[4,128,512]{2,1,0:T(8,128)(2,1)S(1)} %collective-permute-done.12) | copy-start | bytes 1572868
  84.0 14.9 %collective-permute-start.13 = (bf16[4,128,512]{2,1,0:T(8,128)(2,1)S(1)}, bf16[4,128,512]{2,1,0:T(8,128)(2,1)}, u32[]{:S(2)}, u32[]{:S(2)}) collective-permute-start(bf16[4,128,512]{2,1,0:T(8,128)(2,1)S(1)} %collective-permute-done.12), channel_id=1, source_target_pairs={{0,15},{1,0},{2,1},{3,2},{4,3},{5,4},{6,5},{7,6},{8,7},{9,8},{10,9... | collective-permute-start | bytes 1572872 | tf_op jit(solution)/shard_map/ppermute | solution.py:17
  85.6 39.2 %copy-start.18 = (bf16[4,128,512]{2,1,0:T(8,128)(2,1)}, bf16[4,128,512]{2,1,0:T(8,128)(2,1)S(1)}, u32[]{:S(2)}) copy-start(bf16[4,128,512]{2,1,0:T(8,128)(2,1)S(1)} %collective-permute-done.5) | copy-start | bytes 1572868
  85.6 14.3 %collective-permute-start.6 = (bf16[4,128,512]{2,1,0:T(8,128)(2,1)S(1)}, bf16[4,128,512]{2,1,0:T(8,128)(2,1)}, u32[]{:S(2)}, u32[]{:S(2)}) collective-permute-start(bf16[4,128,512]{2,1,0:T(8,128)(2,1)S(1)} %collective-permute-done.5), channel_id=1, source_target_pairs={{0,1},{1,2},{2,3},{3,4},{4,5},{5,6},{6,7},{7,8},{8,9},{9,10},{10,1... | collective-permute-start | bytes 1572872 | tf_op jit(solution)/shard_map/ppermute | solution.py:15
  98.9 57.6 %collective-permute-start.14 = (bf16[4,128,512]{2,1,0:T(8,128)(2,1)}, bf16[4,128,512]{2,1,0:T(8,128)(2,1)}, u32[]{:S(2)}, u32[]{:S(2)}) collective-permute-start(bf16[4,128,512]{2,1,0:T(8,128)(2,1)} %collective-permute-done.13), channel_id=1, source_target_pairs={{0,15},{1,0},{2,1},{3,2},{4,3},{5,4},{6,5},{7,6},{8,7},{9,8},{10,9... | collective-permute-start | bytes 1572872 | tf_op jit(solution)/shard_map/ppermute | solution.py:17
  99.9 40.8 %collective-permute-start.7 = (bf16[4,128,512]{2,1,0:T(8,128)(2,1)}, bf16[4,128,512]{2,1,0:T(8,128)(2,1)}, u32[]{:S(2)}, u32[]{:S(2)}) collective-permute-start(bf16[4,128,512]{2,1,0:T(8,128)(2,1)} %collective-permute-done.6), channel_id=1, source_target_pairs={{0,1},{1,2},{2,3},{3,4},{4,5},{5,6},{6,7},{7,8},{8,9},{9,10},{10,1... | collective-permute-start | bytes 1572872 | tf_op jit(solution)/shard_map/ppermute | solution.py:15
  112.3 12.5 %copy-start.2 = (bf16[128,8192]{1,0:T(8,128)(2,1)S(1)}, bf16[128,8192]{1,0:T(8,128)(2,1)}, u32[]{:S(2)}) copy-start(bf16[128,8192]{1,0:T(8,128)(2,1)} %all-gather.2.cloned.1.call-done) | copy-start | bytes 6291460
  112.3 12.5 %copy-start.20 = (s32[128,1792]{1,0:T(8,128)S(1)}, s32[128,1792]{1,0:T(8,128)}, u32[]{:S(2)}) copy-start(s32[128,1792]{1,0:T(8,128)} %param.13) | copy-start | bytes 2752516
  124.8 19.6 %copy-start.19 = (bf16[4,128,512]{2,1,0:T(8,128)(2,1)S(1)}, bf16[4,128,512]{2,1,0:T(8,128)(2,1)}, u32[]{:S(2)}) copy-start(bf16[4,128,512]{2,1,0:T(8,128)(2,1)} %copy-done.18) | copy-start | bytes 1572868
  124.8 20.5 %copy-start.17 = (bf16[4,128,512]{2,1,0:T(8,128)(2,1)S(1)}, bf16[4,128,512]{2,1,0:T(8,128)(2,1)}, u32[]{:S(2)}) copy-start(bf16[4,128,512]{2,1,0:T(8,128)(2,1)} %copy-done.16) | copy-start | bytes 1572868
  124.8 21.3 %copy-start.15 = (bf16[4,128,512]{2,1,0:T(8,128)(2,1)S(1)}, bf16[4,128,512]{2,1,0:T(8,128)(2,1)}, u32[]{:S(2)}) copy-start(bf16[4,128,512]{2,1,0:T(8,128)(2,1)} %copy-done.14) | copy-start | bytes 1572868
  124.8 22.2 %copy-start.9 = (bf16[4,128,512]{2,1,0:T(8,128)(2,1)S(1)}, bf16[4,128,512]{2,1,0:T(8,128)(2,1)}, u32[]{:S(2)}) copy-start(bf16[4,128,512]{2,1,0:T(8,128)(2,1)} %copy-done.8) | copy-start | bytes 1572868
  124.8 23.0 %copy-start.5 = (bf16[4,128,512]{2,1,0:T(8,128)(2,1)S(1)}, bf16[4,128,512]{2,1,0:T(8,128)(2,1)}, u32[]{:S(2)}) copy-start(bf16[4,128,512]{2,1,0:T(8,128)(2,1)} %copy-done.4) | copy-start | bytes 1572868
  124.9 24.7 %copy-start.3 = (bf16[4,128,512]{2,1,0:T(8,128)(2,1)S(1)}, bf16[4,128,512]{2,1,0:T(8,128)(2,1)}, u32[]{:S(2)}) copy-start(bf16[4,128,512]{2,1,0:T(8,128)(2,1)} %param.11) | copy-start | bytes 1572868
  124.9 27.2 %copy-start.7 = (bf16[4,128,512]{2,1,0:T(8,128)(2,1)S(1)}, bf16[4,128,512]{2,1,0:T(8,128)(2,1)}, u32[]{:S(2)}) copy-start(bf16[4,128,512]{2,1,0:T(8,128)(2,1)} %copy-done.6) | copy-start | bytes 1572868
  124.9 28.1 %copy-start.11 = (bf16[4,128,512]{2,1,0:T(8,128)(2,1)S(1)}, bf16[4,128,512]{2,1,0:T(8,128)(2,1)}, u32[]{:S(2)}) copy-start(bf16[4,128,512]{2,1,0:T(8,128)(2,1)} %copy-done.10) | copy-start | bytes 1572868
  124.9 28.9 %copy-start.13 = (bf16[4,128,512]{2,1,0:T(8,128)(2,1)S(1)}, bf16[4,128,512]{2,1,0:T(8,128)(2,1)}, u32[]{:S(2)}) copy-start(bf16[4,128,512]{2,1,0:T(8,128)(2,1)} %copy-done.12) | copy-start | bytes 1572868
  204.4 0.9 copy-start
  295.7 17.3 %copy-start.1 = (f32[128,1792]{1,0:T(8,128)S(1)}, f32[128,1792]{1,0:T(8,128)}, u32[]{:S(2)}) copy-start(f32[128,1792]{1,0:T(8,128)} %get-tuple-element.10) | copy-start | bytes 2752516
Sparse Core Ops, SparseCore 0:
  10.2 56.2 all-gather.1
  332.3 75.3 reduce-scatter.1
